TPU v7x, 512 devices: a whole 4x4x16 slice. The times are simulated.
512 devices in a mesh: chan: 8 (over y, x_lo), tile: 64 (over z, x_hi, core).
Axes of the slice: x: 4 (x_hi: 2, x_lo: 2; x = x_hi * 2 + x_lo), y: 4, z: 16, core: 2. Of those that a mesh axis runs over, the one named last changes fastest.
Arguments:
- image: bfloat16 [256, 1024, 256], P('chan', 'tile'), may hold values from -6 to 6
- w_down: bfloat16 [2, 2, 256, 512], P(None, None, None, 'chan'), may hold values from -0.1875 to 0.1875
- w_mix: bfloat16 [3, 3, 512, 512], P(None, None, None, 'chan'), may hold values from -0.09375 to 0.09375
- cotangent: bfloat16 [512, 512, 128], P('chan', 'tile'), may hold values from -6 to 6
Outputs:
- mixed: bfloat16 [512, 512, 128], P('chan', 'tile')
- grad_mix: float32 [512, 3, 3, 512], P('tile', None, None, 'chan')
- grad_down: float32 [256, 2, 2, 512], P('tile', None, None, 'chan')
- grad_image: bfloat16 [256, 1024, 256], P('chan', 'tile')
All inputs are finite; a program needn't handle non-finite values.
Results may differ from a plain program's by a relative error of at most 0.0049.
Values may be sent and summed in bfloat16 or wider, within the bound.
No kernel may reach another device: no remote copies, remote signals or barrier semaphores. Data moves between devices by JAX's collectives and lax.ppermute only.
A program may use at most 64 MiB of HBM per device.

v0:
```python
import math
import jax
import jax.numpy as jnp
from jax import lax
from jax.sharding import PartitionSpec as P


def with_halo(block, sides, width):
    for axis, dim in sides:
        count = lax.axis_size(axis)
        forward = [(i, i + 1) for i in range(count - 1)]
        backward = [(target, source) for source, target in forward]
        low = lax.ppermute(
            lax.slice_in_dim(block, block.shape[dim] - width, None, axis=dim), axis, forward
        )
        high = lax.ppermute(lax.slice_in_dim(block, 0, width, axis=dim), axis, backward)
        block = jnp.concatenate([low, block, high], axis=dim)
    return block


def normal_cdf(value):
    return 0.5 * (1.0 + jax.scipy.special.erf(value / math.sqrt(2.0)))


def normal_pdf(value):
    return jnp.exp(-0.5 * value * value) / math.sqrt(2.0 * math.pi)


def per_device(image, w_down, w_mix, cotangent):
    n_tile = lax.axis_size("tile")
    own_out = cotangent.shape[0]
    n_rows = cotangent.shape[1]
    n_cols = cotangent.shape[2]
    own_in = image.shape[0]
    scale = 1.0 / math.sqrt(n_rows * n_tile * n_cols)
    wide_image = lax.all_gather(image, "chan", axis=0, tiled=True)
    in_chan = wide_image.shape[0]
    patches = wide_image.reshape(in_chan, n_rows, 2, n_cols, 2)
    preact = jnp.einsum("crawb,abcd->drw", patches, w_down, preferred_element_type=jnp.float32)
    hidden = (preact * normal_cdf(preact)).astype(jnp.bfloat16)
    plain = lax.all_gather(hidden, "chan", axis=0, tiled=True)
    full_hidden = with_halo(plain, (("tile", 1),), 1)
    hidden_pad = jnp.pad(full_hidden, ((0, 0), (0, 0), (1, 1)))
    all_chan = hidden_pad.shape[0]
    mixed_sum = jnp.zeros((own_out, n_rows, n_cols), jnp.float32)
    for tap_row in range(3):
        for tap_col in range(3):
            window = hidden_pad[:, tap_row : tap_row + n_rows, tap_col : tap_col + n_cols]
            mixed_sum = mixed_sum + jnp.einsum(
                "crw,cd->drw", window, w_mix[tap_row, tap_col], preferred_element_type=jnp.float32
            )
    mixed = mixed_sum.astype(jnp.bfloat16)
    cot_rimmed = with_halo(cotangent, (("tile", 1),), 1)
    part = hidden_pad
    terms = []
    for tap_row in range(3):
        for tap_col in range(3):
            window = part[:, tap_row : tap_row + n_rows, tap_col : tap_col + n_cols]
            terms.append(
                jnp.einsum("crw,drw->cd", window, cotangent, preferred_element_type=jnp.float32)
            )
    grad_mix = (
        lax.psum_scatter(
            jnp.stack(terms, 1).reshape(all_chan // n_tile * lax.axis_size("tile"), 3, 3, own_out),
            "tile",
            scatter_dimension=0,
            tiled=True,
        )
        * scale
    )
    cot_pad = jnp.pad(cot_rimmed, ((0, 0), (0, 0), (1, 1)))
    total = jnp.zeros((own_out * lax.axis_size("chan"), n_rows, n_cols), jnp.float32)
    for tap_row in range(3):
        for tap_col in range(3):
            back = cot_pad[
                :, 2 - tap_row : 2 - tap_row + n_rows, 2 - tap_col : 2 - tap_col + n_cols
            ]
            filters = w_mix[tap_row, tap_col]
            total = total + jnp.einsum(
                "drw,cd->crw", back, filters, preferred_element_type=jnp.float32
            )
    grad_hidden = lax.psum_scatter(total, "chan", scatter_dimension=0, tiled=True)
    slope = normal_cdf(preact) + preact * normal_pdf(preact)
    grad_pre = (grad_hidden * slope).astype(jnp.bfloat16)
    part = patches
    grad_down = (
        lax.psum_scatter(
            jnp.einsum("crawb,drw->cabd", part, grad_pre, preferred_element_type=jnp.float32),
            "tile",
            scatter_dimension=0,
            tiled=True,
        )
        * scale
    )
    down_turned = lax.all_to_all(w_down, "chan", split_axis=2, concat_axis=3, tiled=True)
    filters = down_turned
    term = jnp.einsum(
        "drw,abcd->crawb",
        lax.all_gather(grad_pre, "chan", axis=0, tiled=True),
        filters,
        preferred_element_type=jnp.float32,
    )
    grad_image = term.reshape(jnp.zeros((own_in, 2 * n_rows, 2 * n_cols), jnp.float32).shape)
    return (mixed, grad_mix, grad_down, grad_image.astype(jnp.bfloat16))


def solution(mesh):
    return jax.shard_map(
        per_device,
        mesh=mesh,
        in_specs=(
            P("chan", "tile", None),
            P(None, None, None, "chan"),
            P(None, None, None, "chan"),
            P("chan", "tile", None),
        ),
        out_specs=(
            P("chan", "tile", None),
            P("tile", None, None, "chan"),
            P("tile", None, None, "chan"),
            P("chan", "tile", None),
        ),
        check_vma=False,
    )
```

profile of v0, /device:TPU:8, one launch (start us, length us, event | category | flops | bytes accessed | tf_op | source)
XLA Modules:
  0.0 1003.0 jit_solution(11535265165605964177)
XLA Ops:
  8.9 1.7 collective-permute-start.2
  11.9 1.4 fusion.96
  13.4 3.2 collective-permute-done.3
  20.2 2.6 bitcast_add_fusion
  22.9 49.7 %all-gather.4.cloned.1.call-done = bf16[256,16,256]{2,1,0:T(8,128)(2,1)} async-done(((bf16[32,16,256]{2,1,0:T(8,128)(2,1)}), bf16[256,16,256]{2,1,0:T(8,128)(2,1)}) %all-gather.4.cloned.1.call-update) | async-done | bytes 2097168 | tf_op jit(solution)/shard_map/all_gather | solution.py:36
  72.6 3.0 copy.69
  75.6 2.2 reshape.16
  77.8 2.5 fusion.11
  80.3 54.6 %reduce-scatter.5.cloned.1.call-done = f32[64,8,128]{2,0,1:T(8,128)} async-done(((f32[512,8,128]{2,0,1:T(8,128)}), f32[64,8,128]{2,0,1:T(8,128)}) %reduce-scatter.5.cloned.1.call-update) | async-done | bytes 262160 | tf_op jit(solution)/shard_map/reduce_scatter | solution.py:82
  134.9 1.7 fusion.66
  140.4 5.5 all-to-all-start
  147.8 3.2 all-to-all-done
  151.6 511.6 %all-reduce.5.cloned.1.call-done = f32[256,2,2,64]{3,2,1,0:T(2,128)} async-done(((f32[256,2,2,64]{3,2,1,0:T(2,128)}), f32[256,2,2,64]{3,2,1,0:T(2,128)}) %all-reduce.5.cloned.1.call-update) | async-done | bytes 262160
  663.2 1.3 dynamic-slice_multiply_fusion
  664.5 47.3 %all-gather.6.cloned.1.call-done = bf16[512,8,128]{2,0,1:T(8,128)(2,1)} async-done(((bf16[64,8,128]{2,0,1:T(8,128)(2,1)}), bf16[512,8,128]{2,0,1:T(8,128)(2,1)}) %all-gather.6.cloned.1.call-update) | async-done | bytes 1048592 | tf_op jit(solution)/shard_map/all_gather | solution.py:41
  711.9 1.6 fusion.138
  713.5 1.4 collective-permute-start
  714.9 1.5 collective-permute-start.1
  716.4 45.3 %all-gather.8.cloned.1.call-done = bf16[512,8,128]{2,0,1:T(8,128)(2,1)} async-done(((bf16[64,8,128]{2,0,1:T(8,128)(2,1)}), bf16[512,8,128]{2,0,1:T(8,128)(2,1)}) %all-gather.8.cloned.1.call-update) | async-done | bytes 1048592 | tf_op jit(solution)/shard_map/all_gather | solution.py:99
  761.7 1.5 fusion.10
  766.2 2.9 fusion.5
  777.9 2.9 copy.80
  784.8 209.9 %reduce-scatter.3.cloned.1.call-done = f32[8,3,3,64]{3,0,2,1:T(8,128)} async-done(((f32[512,3,3,64]{3,0,2,1:T(8,128)}), f32[8,3,3,64]{3,0,2,1:T(8,128)}) %reduce-scatter.3.cloned.1.call-update) | async-done | bytes 18448 | tf_op jit(solution)/shard_map/reduce_scatter | solution.py:63
  994.7 1.4 broadcast_multiply_fusion
  (85 shorter events, 27.7 us)
Async XLA Ops:
  7.2 9.6 copy-start.5
  7.2 65.4 %all-gather.4.cloned.1.call-start = ((), (), s32[]{:S(2)}) async-start(), calls=%async_computation.3 | async-start | bytes 2359296 | tf_op jit(solution)/shard_map/all_gather | solution.py:36
  7.9 127.0 %reduce-scatter.5.cloned.1.call-start = ((), (), s32[]{:S(2)}) async-start(), calls=%async_computation.6 | async-start | bytes 2359296 | tf_op jit(solution)/shard_map/reduce_scatter | solution.py:82
  8.9 4.4 collective-permute-start.2
  10.6 5.9 collective-permute-start.3
  22.8 640.4 %all-reduce.5.cloned.1.call-start = ((), (), s32[]{:S(2)}) async-start(), calls=%async_computation.8 | async-start | bytes 1048576
  75.6 2.2 copy-start.12
  77.8 58.9 %copy-start.6 = (bf16[256,8,2,128,2]{0,4,3,2,1:T(2,128)(2,1)S(1)}, bf16[256,8,2,128,2]{0,4,3,2,1:T(2,128)(2,1)}, u32[]{:S(2)}) copy-start(bf16[256,8,2,128,2]{0,4,3,2,1:T(2,128)(2,1)} %reshape.16) | copy-start | bytes 6291460
  136.7 2.1 copy-start.11
  138.2 573.7 %all-gather.6.cloned.1.call-start = ((), (), s32[]{:S(2)}) async-start(), calls=%async_computation.4 | async-start | bytes 1179648 | tf_op jit(solution)/shard_map/all_gather | solution.py:41
  138.8 623.0 %all-gather.8.cloned.1.call-start = ((), (), s32[]{:S(2)}) async-start(), calls=%async_computation.7 | async-start | bytes 1179648 | tf_op jit(solution)/shard_map/all_gather | solution.py:99
  140.4 10.6 %all-to-all-start = ((bf16[8,2,4096]{2,1,0:T(2,128)(2,1)}), bf16[8,2,4096]{2,1,0:T(2,128)(2,1)S(1)}, u32[]{:S(2)}, u32[]{:S(2)}) async-start(bf16[8,2,4096]{2,1,0:T(2,128)(2,1)} %reshape.44), calls=%async_computation.2 | async-start | bytes 262144 | tf_op jit(solution)/shard_map/all_to_all | solution.py:95
  145.9 848.8 %reduce-scatter.3.cloned.1.call-start = ((), (), s32[]{:S(2)}) async-start(), calls=%async_computation.5 | async-start | bytes 2396160 | tf_op jit(solution)/shard_map/reduce_scatter | solution.py:63
  713.5 51.7 %copy-start = (bf16[512,8,128]{2,0,1:T(8,128)(2,1)S(1)}, bf16[512,8,128]{2,0,1:T(8,128)(2,1)}, u32[]{:S(2)}) copy-start(bf16[512,8,128]{2,0,1:T(8,128)(2,1)} %all-gather.6.cloned.1.call-done) | copy-start | bytes 3145732
  713.5 52.0 %collective-permute-start = (bf16[512,1,128]{2,0,1:T(8,128)(2,1)}, bf16[512,1,128]{2,0,1:T(8,128)(2,1)S(1)}, u32[]{:S(2)}, u32[]{:S(2)}) collective-permute-start(bf16[512,1,128]{2,0,1:T(8,128)(2,1)} %get-tuple-element.18), channel_id=1, source_target_pairs={{0,1},{1,2},{2,3},{3,4},{4,5},{5,6},{6,7},{7,8},{8,9},{9,10},{10,1... | collective-permute-start | bytes 393224 | tf_op jit(solution)/shard_map/ppermute | solution.py:13
  714.9 51.3 %collective-permute-start.1 = (bf16[512,1,128]{2,0,1:T(8,128)(2,1)S(1)}, bf16[512,1,128]{2,0,1:T(8,128)(2,1)}, u32[]{:S(2)}, u32[]{:S(2)}) collective-permute-start(bf16[512,1,128]{2,0,1:T(8,128)(2,1)S(1)} %get-tuple-element.19), channel_id=1, source_target_pairs={{1,0},{2,1},{3,2},{4,3},{5,4},{6,5},{7,6},{8,7},{9,8},{10,9},{11,1... | collective-permute-start | bytes 393224 | tf_op jit(solution)/shard_map/ppermute | solution.py:16
  765.5 3.6 copy-start.4
  765.5 4.1 copy-start.1
  765.5 0.7 copy-start.9
  766.2 3.4 copy-start.10
  774.8 1.0 copy-start.2
  776.8 1.0 copy-start.7
  780.8 1.3 copy-start.3
  782.0 1.2 copy-start.8
Sparse Core Ops, SparseCore 0:
  10.1 62.4 all-gather.3
  75.4 59.4 reduce-scatter.4
  138.3 524.8 all-reduce.4
  665.9 45.8 all-gather.5
  714.0 47.6 all-gather.7
  780.9 213.8 reduce-scatter.2
where the time goes:
time: 1000 us
  waiting for transfers between devices  927 us (93%)
  local copies, waits for them, and re-layouts  21.7 us (2%)
  matrix products  20.4 us (2%)
  between operations  15.1 us (2%)
  starting transfers between devices  11.6 us (1%)
    unnamed x7, waiting for transfers between devices  513 us
    reduce_scatter x1, waiting for transfers between devices, per_device(): lax.psum_scatter(jnp.stack(terms, 1).reshape(all_chan // n_tile * lax.axi...  210 us
    reduce_scatter x1, waiting for transfers between devices, per_device(): lax.psum_scatter(total, 'chan', scatter_dimension=0, tiled=True)  54.6 us
    all_gather x1, waiting for transfers between devices, per_device(): wide_image = lax.all_gather(image, 'chan', axis=0, tiled=True)  49.7 us
    all_gather x1, waiting for transfers between devices, per_device(): plain = lax.all_gather(hidden, 'chan', axis=0, tiled=True)  47.3 us
    all_gather x1, waiting for transfers between devices, per_device(): lax.all_gather(grad_pre, 'chan', axis=0, tiled=True)  45.3 us
  transfers between devices with their start and end apart: 11, of which 8 were waited for; matrix products, arithmetic and copies ran while one was open for 3% of the time, Pallas kernels for 0%

commit v1 on v0

--- a/solution.py
+++ b/solution.py
@@ -96,7 +96,9 @@
     filters = down_turned
     term = jnp.einsum(
         "drw,abcd->crawb",
-        lax.all_gather(grad_pre, "chan", axis=0, tiled=True),
+        jnp.concatenate(
+            lax.all_to_all(jnp.stack([grad_pre] * lax.axis_size("chan")), "chan", 0, 0), axis=0
+        ),
         filters,
         preferred_element_type=jnp.float32,
     )

time: 1000 us -> 960 us (0.960)
  waiting for transfers between devices: 927 us -> 877 us
  blocking collectives: 0 us -> 10.3 us
    all_gather x1 -> x0, waiting for transfers between devices: 45.3 us -> none  [per_device(): lax.all_gather(grad_pre, 'chan', axis=0, tiled=True)]
    all_to_all x0 -> x1, blocking collectives: none -> 10.3 us  [per_device(): lax.all_to_all(w_down, 'chan', split_axis=2, concat_axis=3, tiled=True)]
    unnamed x7 -> x6, waiting for transfers between devices: 513 us -> 507 us
  transfers between devices with their start and end apart: 11 -> 10, of which waited for: 8 -> 7; matrix products, arithmetic and copies ran while one was open for 3% -> 3% of each run, Pallas kernels for 0% -> 0%
where the time goes in v1:
time: 960 us
  waiting for transfers between devices  877 us (91%)
  matrix products  20.4 us (2%)
  local copies, waits for them, and re-layouts  19.7 us (2%)
  between operations  14.8 us (2%)
  starting transfers between devices  11.1 us (1%)
  blocking collectives  10.3 us (1%)
    unnamed x6, waiting for transfers between devices  507 us
    reduce_scatter x1, waiting for transfers between devices, per_device(): lax.psum_scatter(jnp.stack(terms, 1).reshape(all_chan // n_tile * lax.axi...  215 us
    reduce_scatter x1, waiting for transfers between devices, per_device(): lax.psum_scatter(total, 'chan', scatter_dimension=0, tiled=True)  54.7 us
    all_gather x1, waiting for transfers between devices, per_device(): wide_image = lax.all_gather(image, 'chan', axis=0, tiled=True)  49.7 us
    all_gather x1, waiting for transfers between devices, per_device(): plain = lax.all_gather(hidden, 'chan', axis=0, tiled=True)  45 us
  transfers between devices with their start and end apart: 10, of which 7 were waited for; matrix products, arithmetic and copies ran while one was open for 3% of the time, Pallas kernels for 0%

profile of v1, /device:TPU:8, one launch (start us, length us, event | category | flops | bytes accessed | tf_op | source)
XLA Modules:
  0.0 959.6 jit_solution(10420794715732392122)
XLA Ops:
  8.9 1.7 collective-permute-start.2
  10.6 1.3 collective-permute-start.3
  11.9 1.4 fusion.97
  13.4 3.2 collective-permute-done.3
  20.2 2.6 bitcast_add_fusion
  22.9 49.7 %all-gather.3.cloned.1.call-done = bf16[256,16,256]{2,1,0:T(8,128)(2,1)} async-done(((bf16[32,16,256]{2,1,0:T(8,128)(2,1)}), bf16[256,16,256]{2,1,0:T(8,128)(2,1)}) %all-gather.3.cloned.1.call-update) | async-done | bytes 2097168 | tf_op jit(solution)/shard_map/all_gather | solution.py:36
  72.6 3.0 copy.68
  75.6 2.2 reshape.19
  77.8 2.5 fusion.12
  80.3 54.7 %reduce-scatter.5.cloned.1.call-done = f32[64,8,128]{2,0,1:T(8,128)} async-done(((f32[512,8,128]{2,0,1:T(8,128)}), f32[64,8,128]{2,0,1:T(8,128)}) %reduce-scatter.5.cloned.1.call-update) | async-done | bytes 262160 | tf_op jit(solution)/shard_map/reduce_scatter | solution.py:82
  134.9 1.7 fusion.67
  139.2 10.3 %all_to_all.20 = bf16[8,2,4096]{2,1,0:T(2,128)(2,1)S(1)} all-to-all(bf16[8,2,4096]{2,1,0:T(2,128)(2,1)S(1)} %reshape.47), channel_id=1, replica_groups=mesh['chan'=8,'tile'=64] {'chan'}, dimensions={0} | all-to-all | bytes 262144 | tf_op jit(solution)/shard_map/all_to_all | solution.py:95
  150.7 5.1 all-to-all-start
  158.0 505.2 %all-reduce.5.cloned.1.call-done = f32[256,2,2,64]{3,2,1,0:T(2,128)} async-done(((f32[256,2,2,64]{3,2,1,0:T(2,128)}), f32[256,2,2,64]{3,2,1,0:T(2,128)}) %all-reduce.5.cloned.1.call-update) | async-done | bytes 262160
  663.2 1.3 dynamic-slice_multiply_fusion
  666.8 45.0 %all-gather.5.cloned.1.call-done = bf16[512,8,128]{2,0,1:T(8,128)(2,1)} async-done(((bf16[64,8,128]{2,0,1:T(8,128)(2,1)}), bf16[512,8,128]{2,0,1:T(8,128)(2,1)}) %all-gather.5.cloned.1.call-update) | async-done | bytes 1048592 | tf_op jit(solution)/shard_map/all_gather | solution.py:41
  712.9 1.3 collective-permute-start
  714.3 1.5 collective-permute-start.1
  715.7 1.5 fusion.99
  717.3 3.1 collective-permute-done.1
  720.4 1.8 fusion.5
  730.0 2.8 copy.79
  736.9 214.8 %reduce-scatter.3.cloned.1.call-done = f32[8,3,3,64]{3,0,2,1:T(8,128)} async-done(((f32[512,3,3,64]{3,0,2,1:T(8,128)}), f32[8,3,3,64]{3,0,2,1:T(8,128)}) %reduce-scatter.3.cloned.1.call-update) | async-done | bytes 18448 | tf_op jit(solution)/shard_map/reduce_scatter | solution.py:63
  951.7 1.4 broadcast_multiply_fusion
  (74 shorter events, 25.7 us)
Async XLA Ops:
  7.2 9.6 copy-start.4
  7.2 65.4 %all-gather.3.cloned.1.call-start = ((), (), s32[]{:S(2)}) async-start(), calls=%async_computation.4 | async-start | bytes 2359296 | tf_op jit(solution)/shard_map/all_gather | solution.py:36
  7.9 127.0 %reduce-scatter.5.cloned.1.call-start = ((), (), s32[]{:S(2)}) async-start(), calls=%async_computation.7 | async-start | bytes 2359296 | tf_op jit(solution)/shard_map/reduce_scatter | solution.py:82
  8.9 4.4 collective-permute-start.2
  10.6 5.9 collective-permute-start.3
  22.8 640.4 %all-reduce.5.cloned.1.call-start = ((), (), s32[]{:S(2)}) async-start(), calls=%async_computation.8 | async-start | bytes 1048576
  75.6 2.2 copy-start.8
  77.8 58.9 %copy-start.5 = (bf16[256,8,2,128,2]{0,4,3,2,1:T(2,128)(2,1)S(1)}, bf16[256,8,2,128,2]{0,4,3,2,1:T(2,128)(2,1)}, u32[]{:S(2)}) copy-start(bf16[256,8,2,128,2]{0,4,3,2,1:T(2,128)(2,1)} %reshape.19) | copy-start | bytes 6291460
  138.2 573.7 %all-gather.5.cloned.1.call-start = ((), (), s32[]{:S(2)}) async-start(), calls=%async_computation.5 | async-start | bytes 1179648 | tf_op jit(solution)/shard_map/all_gather | solution.py:41
  150.7 513.8 %all-to-all-start = ((bf16[8,64,8,128]{3,1,2,0:T(8,128)(2,1)}), bf16[8,64,8,128]{3,1,2,0:T(8,128)(2,1)S(1)}, u32[]{:S(2)}, u32[]{:S(2)}) async-start(bf16[8,64,8,128]{3,1,2,0:T(8,128)(2,1)} %stack.51), calls=%async_computation.2 | async-start | bytes 2097152 | tf_op jit(solution)/shard_map/all_to_all | solution.py:100
  155.8 795.9 %reduce-scatter.3.cloned.1.call-start = ((), (), s32[]{:S(2)}) async-start(), calls=%async_computation.6 | async-start | bytes 2396160 | tf_op jit(solution)/shard_map/reduce_scatter | solution.py:63
  711.9 8.5 copy-start
  712.9 4.3 collective-permute-start
  714.3 6.2 collective-permute-start.1
  717.3 4.9 copy-start.3
  726.9 1.0 copy-start.1
  728.9 1.0 copy-start.6
  732.8 1.3 copy-start.2
  734.1 1.2 copy-start.7
Sparse Core Ops, SparseCore 0:
  10.1 62.4 all-gather.2
  75.4 59.4 reduce-scatter.4
  138.3 524.8 all-reduce.4
  666.0 45.8 all-gather.4
  732.9 218.7 reduce-scatter.2
